TPU v7x, 32 devices: a whole 2x2x4 slice. The times are simulated.
32 devices in a mesh: frame: 4 (over z), pipe: 4 (over x, core), dp: 2 (over y).
Axes of the slice: x: 2, y: 2, z: 4, core: 2. Of those that a mesh axis runs over, the one named last changes fastest.
Arguments:
- acts: bfloat16 [4, 2, 32, 4, 1280], P('pipe', 'dp', 'frame'), may hold values from -18 to 18
- cotangent: bfloat16 [4, 2, 32, 4, 1280], P('pipe', 'dp', 'frame'), may hold values from -6 to 6
- w_query: bfloat16 [4, 1280, 768], P('pipe'), may hold values from -0.15625 to 0.15625
- w_key: bfloat16 [4, 1280, 768], P('pipe'), may hold values from -0.15625 to 0.15625
- w_value: bfloat16 [4, 1280, 768], P('pipe'), may hold values from -0.15625 to 0.15625
- w_out: bfloat16 [4, 1280, 768], P('pipe'), may hold values from -0.21875 to 0.21875
Outputs:
- sent_grad: bfloat16 [4, 2, 32, 4, 1280], P('pipe', 'dp', 'frame')
- grad_value: float32 [4, 1280, 768], P('pipe', None, ('frame', 'dp'))
All inputs are finite; a program needn't handle non-finite values.
Results may differ from a plain program's by a relative error of at most 0.017.
The roundings to bfloat16 on the way count: a program that leaves them out, or rounds other values in their place, can miss the bound.
Values may be sent and summed in bfloat16 or wider, within the bound.
No kernel may reach another device: no remote copies, remote signals or barrier semaphores. Data moves between devices by JAX's collectives and lax.ppermute only.
A program may use at most 64 MiB of HBM per device.

v0:
```python
import jax
import jax.numpy as jnp
from jax import lax
from jax.sharding import PartitionSpec as P

HEADS = 12
HEAD_DIM = 64
score_scale = 0.125


def shifted(shard, axis, by):
    count = lax.axis_size(axis)
    pairs = [(i, i + by) for i in range(count) if 0 <= i + by < count]
    return lax.ppermute(shard, axis, pairs)


def attend_back(inputs, projected, w_query, w_key, w_value):
    frames = inputs.shape[0]
    places = inputs.shape[1]

    def project_heads(weight):
        result = jnp.dot(inputs, weight, preferred_element_type=jnp.float32).astype(jnp.bfloat16)
        return result.reshape(frames, places, HEADS, HEAD_DIM)

    queries = project_heads(w_query)
    key_rows = project_heads(w_key)
    values = project_heads(w_value)
    scores = (
        jnp.einsum("iphd,jphd->phij", queries, key_rows, preferred_element_type=jnp.float32)
        * score_scale
    )
    probability = jax.nn.softmax(scores, axis=-1)
    prob_short = probability.astype(jnp.bfloat16)
    proj_heads = projected.reshape(frames, places, HEADS, HEAD_DIM)
    grad_prob = jnp.einsum(
        "iphd,jphd->phij", proj_heads, values, preferred_element_type=jnp.float32
    )
    value_grad = jnp.einsum(
        "phij,iphd->jphd", prob_short, proj_heads, preferred_element_type=jnp.float32
    ).astype(jnp.bfloat16)
    score_grad = probability * (
        grad_prob - jnp.sum(grad_prob * probability, axis=-1, keepdims=True)
    )
    score_short = score_grad.astype(jnp.bfloat16)
    query_grad = (
        jnp.einsum("phij,jphd->iphd", score_short, key_rows, preferred_element_type=jnp.float32)
        * score_scale
    ).astype(jnp.bfloat16)
    key_grad = (
        jnp.einsum("phij,iphd->jphd", score_short, queries, preferred_element_type=jnp.float32)
        * score_scale
    ).astype(jnp.bfloat16)
    inner = HEADS * HEAD_DIM
    query_grad = query_grad.reshape(frames, places, inner)
    key_grad = key_grad.reshape(frames, places, inner)
    value_grad = value_grad.reshape(frames, places, inner)
    branch = jnp.einsum("fpj,cj->fpc", query_grad, w_query, preferred_element_type=jnp.float32)
    branch = branch + jnp.einsum("fpj,cj->fpc", key_grad, w_key, preferred_element_type=jnp.float32)
    branch = branch + jnp.einsum(
        "fpj,cj->fpc", value_grad, w_value, preferred_element_type=jnp.float32
    )
    branch = branch.astype(jnp.bfloat16)
    weight_grad = jnp.einsum("fpc,fpj->cj", inputs, value_grad, preferred_element_type=jnp.float32)
    return (branch, weight_grad)


def body(acts, cotangent, w_query, w_key, w_value, w_out):
    inputs = acts[0, 0]
    upstream = cotangent[0, 0]
    query_weight = w_query[0]
    key_weight = w_key[0]
    value_weight = w_value[0]
    out_weight = w_out[0]
    row_inputs, row_upstream = (
        lax.all_to_all(inputs, "frame", split_axis=1, concat_axis=0, tiled=True),
        lax.all_to_all(upstream, "frame", split_axis=1, concat_axis=0, tiled=True),
    )
    projected = jnp.dot(row_upstream, out_weight, preferred_element_type=jnp.float32).astype(
        jnp.bfloat16
    )
    branch, value_grad = attend_back(row_inputs, projected, query_weight, key_weight, value_weight)
    row_result = (row_upstream.astype(jnp.float32) + branch.astype(jnp.float32)).astype(
        jnp.bfloat16
    )
    frame_result = lax.all_to_all(row_result, "frame", split_axis=0, concat_axis=1, tiled=True)
    sent_grad = shifted(frame_result[None, None], "pipe", -1)
    value_middle = lax.psum_scatter(
        value_grad.astype(jnp.bfloat16), "frame", scatter_dimension=1, tiled=True
    )
    value_part = lax.psum_scatter(value_middle, "dp", scatter_dimension=1, tiled=True).astype(
        jnp.float32
    )
    return (sent_grad, value_part[None])


def solution(mesh):
    return jax.shard_map(
        body,
        mesh=mesh,
        in_specs=(
            P("pipe", "dp", "frame", None, None),
            P("pipe", "dp", "frame", None, None),
            P("pipe", None, None),
            P("pipe", None, None),
            P("pipe", None, None),
            P("pipe", None, None),
        ),
        out_specs=(P("pipe", "dp", "frame", None, None), P("pipe", None, ("frame", "dp"))),
        check_vma=False,
    )
```

profile of v0, /device:TPU:1, one launch (start us, length us, event | category | flops | bytes accessed | tf_op | source)
XLA Modules:
  0.0 102.3 jit_solution(5683003131072736057)
XLA Ops:
  7.2 1.7 %copy.98 = bf16[1,1,8,4,1280]{4,2,3,1,0:T(8,128)(2,1)} copy(bf16[1,1,8,4,1280]{4,3,2,1,0:T(4,128)(2,1)} %param.6) | data formatting | bytes 163840 | tf_op args[0]
  8.9 5.4 %all-to-all-start.1 = ((bf16[8,4,1280]{2,0,1:T(8,128)(2,1)}), bf16[8,4,1280]{2,0,1:T(8,128)(2,1)S(1)}, u32[]{:S(2)}, u32[]{:S(2)}) async-start(bf16[8,4,1280]{2,0,1:T(8,128)(2,1)} %bitcast.89), calls=%async_computation.1 | async-start | bytes 163840 | tf_op jit(solution)/shard_map/all_to_all | solution.py:75
  14.3 1.5 %copy.99 = bf16[1,1,8,4,1280]{4,2,3,1,0:T(8,128)(2,1)} copy(bf16[1,1,8,4,1280]{4,3,2,1,0:T(4,128)(2,1)} %param.7) | data formatting | bytes 163840 | tf_op args[1]
  15.8 3.1 %all-to-all-done.1 = bf16[8,4,1280]{2,0,1:T(8,128)(2,1)S(1)} async-done(((bf16[8,4,1280]{2,0,1:T(8,128)(2,1)}), bf16[8,4,1280]{2,0,1:T(8,128)(2,1)S(1)}, u32[]{:S(2)}, u32[]{:S(2)}) %all-to-all-start.1) | async-done | bytes 81952 | tf_op jit(solution)/shard_map/all_to_all | solution.py:75
  18.9 3.3 %all-to-all-start = ((bf16[8,4,1280]{2,0,1:T(8,128)(2,1)}), bf16[8,4,1280]{2,0,1:T(8,128)(2,1)S(1)}, u32[]{:S(2)}, u32[]{:S(2)}) async-start(bf16[8,4,1280]{2,0,1:T(8,128)(2,1)} %bitcast.90), calls=%async_computation | async-start | bytes 163840 | tf_op jit(solution)/shard_map/all_to_all | solution.py:76
  22.3 0.5 fusion.29
  22.7 1.1 %copy-done.1 = bf16[1,1280,768]{2,1,0:T(8,128)(2,1)S(1)} copy-done((bf16[1,1280,768]{2,1,0:T(8,128)(2,1)S(1)}, bf16[1,1280,768]{2,1,0:T(8,128)(2,1)}, u32[]{:S(2)}) %copy-start.1) | copy-done | bytes 1966104
  23.8 0.5 fusion.26
  24.3 0.1 reshape.127
  24.6 2.2 %all-to-all-done = bf16[8,4,1280]{2,0,1:T(8,128)(2,1)S(1)} async-done(((bf16[8,4,1280]{2,0,1:T(8,128)(2,1)}), bf16[8,4,1280]{2,0,1:T(8,128)(2,1)S(1)}, u32[]{:S(2)}, u32[]{:S(2)}) %all-to-all-start) | async-done | bytes 81952 | tf_op jit(solution)/shard_map/all_to_all | solution.py:76
  26.8 2.0 %fusion.32 = bf16[32,768]{1,0:T(8,128)(2,1)S(1)} fusion(bf16[1,1280,768]{2,1,0:T(8,128)(2,1)} %param.11, bf16[8,4,1280]{2,0,1:T(8,128)(2,1)S(1)} %all-to-all-done), kind=kOutput, calls=%fused_computation.35 | convolution fusion | flops 62939136 | bytes 2097152 | tf_op jit(solution)/shard_map/dot_general | solution.py:78
  28.8 0.1 reshape.129
  29.0 0.2 fusion.62
  29.2 0.2 fusion.23
  29.5 2.0 %fusion.1 = bf16[1280,768]{0,1:T(8,128)(2,1)} fusion(bf16[32,768]{1,0:T(8,128)(2,1)S(1)} %reshape.133, bf16[8,4,1280]{2,0,1:T(8,128)(2,1)S(1)} %all-to-all-done.1), kind=kOutput, calls=%fused_computation.2 | convolution fusion | flops 63897600 | bytes 2097152 | tf_op jit(solution)/shard_map/fpc,fpj->cj/dot_general | solution.py:63
  31.6 2.0 %fusion.35 = bf16[32,768]{1,0:T(8,128)(2,1)S(1)} fusion(bf16[1,1280,768]{2,1,0:T(8,128)(2,1)} %param.10, bf16[8,4,1280]{2,0,1:T(8,128)(2,1)S(1)} %all-to-all-done.1), kind=kOutput, calls=%fused_computation.36 | convolution fusion | flops 62939136 | bytes 2097152 | tf_op jit(solution)/shard_map/dot_general | solution.py:22
  33.6 0.1 reshape.130
  33.8 0.2 multiply_reduce_fusion
  34.0 0.2 fusion.25
  34.4 0.2 fusion.24
  34.8 39.4 %reduce-scatter.3.cloned.1.call-done = bf16[1280,192]{0,1:T(8,128)(2,1)} async-done(((bf16[1280,768]{0,1:T(8,128)(2,1)}), bf16[1280,192]{0,1:T(8,128)(2,1)}) %reduce-scatter.3.cloned.1.call-update) | async-done | bytes 491536 | tf_op jit(solution)/shard_map/reduce_scatter | solution.py:87
  74.2 0.7 fusion.12
  74.9 0.8 copy-done.2
  75.7 0.7 convolution_add_fusion.1
  76.4 0.7 fusion.6
  77.1 0.5 broadcast.23
  77.7 0.7 reduce.6
  78.4 7.6 %all_to_all.48 = bf16[4,2,5120]{2,1,0:T(2,128)(2,1)S(1)} all-to-all(bf16[4,2,5120]{2,1,0:T(2,128)(2,1)S(1)} %reshape.135), channel_id=1, replica_groups=mesh['frame'=4,'pipe'=4,'dp'=2] {'frame'}, dimensions={0} | all-to-all | bytes 163840 | tf_op jit(solution)/shard_map/all_to_all | solution.py:85
  86.1 3.9 %collective-permute-start = (bf16[1,1,8,4,1280]{4,2,3,1,0:T(8,128)(2,1)S(1)}, bf16[1,1,8,4,1280]{4,2,3,1,0:T(8,128)(2,1)S(1)}, u32[]{:S(2)}, u32[]{:S(2)}) collective-permute-start(bf16[1,1,8,4,1280]{4,2,3,1,0:T(8,128)(2,1)S(1)} %bitcast.91), channel_id=1, source_target_pairs={{2,0},{4,2},{6,4},{3,1},{5,3},{7,5},{10,8},{12,10},{14,12},{11,9},... | collective-permute-start | bytes 245768 | tf_op jit(solution)/shard_map/ppermute | solution.py:14
  90.0 3.0 %collective-permute-done = bf16[1,1,8,4,1280]{4,2,3,1,0:T(8,128)(2,1)S(1)} collective-permute-done((bf16[1,1,8,4,1280]{4,2,3,1,0:T(8,128)(2,1)S(1)}, bf16[1,1,8,4,1280]{4,2,3,1,0:T(8,128)(2,1)S(1)}, u32[]{:S(2)}, u32[]{:S(2)}) %collective-permute-start) | collective-permute-done | bytes 81952 | tf_op jit(solution)/shard_map/ppermute | solution.py:14
  93.0 0.7 copy.61
  93.7 1.8 %bitcast_convert_fusion = f32[1,1280,96]{1,2,0:T(8,128)} fusion(bf16[1280,96]{0,1:T(8,128)(2,1)} %reduce-scatter.5.cloned.1.call-done), kind=kLoop, calls=%fused_computation.37 | loop fusion | flops 122880 | bytes 737280 | tf_op jit(solution)/shard_map/broadcast_in_dim | solution.py:93
  (22 shorter events, 1.0 us)
Async XLA Ops:
  7.2 15.1 %copy-start = (bf16[1,1280,768]{2,1,0:T(8,128)(2,1)S(1)}, bf16[1,1280,768]{2,1,0:T(8,128)(2,1)}, u32[]{:S(2)}) copy-start(bf16[1,1280,768]{2,1,0:T(8,128)(2,1)} %param.8) | copy-start | bytes 5898244
  8.9 10.0 %all-to-all-start.1 = ((bf16[8,4,1280]{2,0,1:T(8,128)(2,1)}), bf16[8,4,1280]{2,0,1:T(8,128)(2,1)S(1)}, u32[]{:S(2)}, u32[]{:S(2)}) async-start(bf16[8,4,1280]{2,0,1:T(8,128)(2,1)} %bitcast.89), calls=%async_computation.1 | async-start | bytes 163840 | tf_op jit(solution)/shard_map/all_to_all | solution.py:75
  18.9 7.9 %all-to-all-start = ((bf16[8,4,1280]{2,0,1:T(8,128)(2,1)}), bf16[8,4,1280]{2,0,1:T(8,128)(2,1)S(1)}, u32[]{:S(2)}, u32[]{:S(2)}) async-start(bf16[8,4,1280]{2,0,1:T(8,128)(2,1)} %bitcast.90), calls=%async_computation | async-start | bytes 163840 | tf_op jit(solution)/shard_map/all_to_all | solution.py:76
  22.2 51.9 %reduce-scatter.3.cloned.1.call-start = ((), (), s32[]{:S(2)}) async-start(), calls=%async_computation.5 | async-start | bytes 2457600 | tf_op jit(solution)/shard_map/reduce_scatter | solution.py:87
  22.3 1.5 %copy-start.1 = (bf16[1,1280,768]{2,1,0:T(8,128)(2,1)S(1)}, bf16[1,1280,768]{2,1,0:T(8,128)(2,1)}, u32[]{:S(2)}) copy-start(bf16[1,1280,768]{2,1,0:T(8,128)(2,1)} %param.9) | copy-start | bytes 5898244
  31.5 62.2 %reduce-scatter.5.cloned.1.call-start = ((), (), s32[]{:S(2)}) async-start(), calls=%async_computation.6 | async-start | bytes 737280 | tf_op jit(solution)/shard_map/reduce_scatter | solution.py:90
  74.2 1.5 %copy-start.2 = (bf16[1,1280,768]{2,1,0:T(8,128)(2,1)S(1)}, bf16[1,1280,768]{2,1,0:T(8,128)(2,1)}, u32[]{:S(2)}) copy-start(bf16[1,1280,768]{2,1,0:T(8,128)(2,1)} %param.9) | copy-start | bytes 5898244
  74.2 2.2 %copy-start.3 = (bf16[1,1280,768]{2,1,0:T(8,128)(2,1)S(1)}, bf16[1,1280,768]{2,1,0:T(8,128)(2,1)}, u32[]{:S(2)}) copy-start(bf16[1,1280,768]{2,1,0:T(8,128)(2,1)} %param.10) | copy-start | bytes 5898244
  86.1 6.9 %collective-permute-start = (bf16[1,1,8,4,1280]{4,2,3,1,0:T(8,128)(2,1)S(1)}, bf16[1,1,8,4,1280]{4,2,3,1,0:T(8,128)(2,1)S(1)}, u32[]{:S(2)}, u32[]{:S(2)}) collective-permute-start(bf16[1,1,8,4,1280]{4,2,3,1,0:T(8,128)(2,1)S(1)} %bitcast.91), channel_id=1, source_target_pairs={{2,0},{4,2},{6,4},{3,1},{5,3},{7,5},{10,8},{12,10},{14,12},{11,9},... | collective-permute-start | bytes 245768 | tf_op jit(solution)/shard_map/ppermute | solution.py:14
Sparse Core Ops, SparseCore 0:
  31.7 42.4 reduce-scatter.2
  76.4 13.5 reduce-scatter.4
where the time goes:
time: 103 us; the launch traced here: 102 us
  waiting for transfers between devices  47.8 us (46%)
  between operations  14.2 us (14%)
  starting transfers between devices  12.7 us (12%)
  matrix products  9.96 us (10%)
  blocking collectives  7.64 us (7%)
  local copies, waits for them, and re-layouts  7.55 us (7%)
  other arithmetic  2.47 us (2%)
    reduce_scatter x1, waiting for transfers between devices, body(): lax.psum_scatter(value_grad.astype(jnp.bfloat16), 'frame', scatter_dimens...  39.4 us
    all_to_all x1, blocking collectives, body(): lax.all_to_all(row_result, 'frame', split_axis=0, concat_axis=1, tiled=True)  7.64 us
    unnamed x14, local copies, waits for them, and re-layouts  5.91 us
    all_to_all x1, starting transfers between devices, body(): lax.all_to_all(inputs, 'frame', split_axis=1, concat_axis=0, tiled=True)  5.41 us
    ppermute x1, starting transfers between devices, shifted(): return lax.ppermute(shard, axis, pairs)  3.88 us
    all_to_all x1, starting transfers between devices, body(): lax.all_to_all(upstream, 'frame', split_axis=1, concat_axis=0, tiled=True)  3.3 us
    all_to_all x1, waiting for transfers between devices, body(): lax.all_to_all(inputs, 'frame', split_axis=1, concat_axis=0, tiled=True)  3.11 us
    ppermute x1, waiting for transfers between devices, shifted(): return lax.ppermute(shard, axis, pairs)  3.04 us
  transfers between devices with their start and end apart: 5, of which 4 were waited for; matrix products, arithmetic and copies ran while one was open for 10% of the time, Pallas kernels for 0%

commit v1 on v0

--- a/solution.py
+++ b/solution.py
@@ -6,6 +6,17 @@
 HEADS = 12
 HEAD_DIM = 64
 score_scale = 0.125
+
+
+def cut_along(x, dim, size):
+    before, after = (x.shape[:dim], x.shape[dim + 1 :])
+    return jnp.moveaxis(x.reshape(*before, size, -1, *after), dim, 0)
+
+
+def laid_out(blocks, dim):
+    lengths = list(blocks.shape[1:])
+    lengths[dim] *= blocks.shape[0]
+    return jnp.moveaxis(blocks, 0, dim).reshape(lengths)
 
 
 def shifted(shard, axis, by):
@@ -82,7 +93,14 @@
     row_result = (row_upstream.astype(jnp.float32) + branch.astype(jnp.float32)).astype(
         jnp.bfloat16
     )
-    frame_result = lax.all_to_all(row_result, "frame", split_axis=0, concat_axis=1, tiled=True)
+    size, position = (lax.axis_size("frame"), lax.axis_index("frame"))
+    blocks = cut_along(row_result, 0, size)
+    done = [blocks[position]]
+    for step in range(1, size):
+        sent = blocks[position ^ step]
+        done.append(lax.ppermute(sent, "frame", [(i_2, i_2 ^ step) for i_2 in range(size)]))
+    blocks = jnp.stack(done)[position ^ jnp.arange(size)]
+    frame_result = laid_out(blocks, 1)
     sent_grad = shifted(frame_result[None, None], "pipe", -1)
     value_middle = lax.psum_scatter(
         value_grad.astype(jnp.bfloat16), "frame", scatter_dimension=1, tiled=True

time: 103 us -> 100 us (0.971)
  blocking collectives: 7.64 us -> 0 us
  starting transfers between devices: 12.7 us -> 16.8 us
  matrix products: 9.96 us -> 11.7 us
    all_to_all x1 -> x0, blocking collectives: 7.64 us -> none  [body(): lax.all_to_all(row_result, 'frame', split_axis=0, concat_axis=1, tiled=True)]
    ppermute x0 -> x3, starting transfers between devices: none -> 3.61 us  [body(): lax.ppermute(sent, 'frame', [(i_2, i_2 ^ step) for i_2 in range(size)])]
    dot_general x1, matrix products: 0.7 us -> 2.39 us  [attend_back(): jnp.einsum('fpj,cj->fpc', key_grad, w_key, preferred_element_type=jnp.flo...]
    ppermute x0 -> x3, waiting for transfers between devices: none -> 1.39 us  [body(): lax.ppermute(sent, 'frame', [(i_2, i_2 ^ step) for i_2 in range(size)])]
    unnamed x14 -> x9, local copies, waits for them, and re-layouts: 5.91 us -> 4.97 us
  transfers between devices with their start and end apart: 5 -> 8, of which waited for: 4 -> 6; matrix products, arithmetic and copies ran while one was open for 10% -> 11% of each run, Pallas kernels for 0% -> 0%
where the time goes in v1:
time: 100 us; the launch traced here: 99.8 us
  waiting for transfers between devices  48.6 us (49%)
  starting transfers between devices  16.8 us (17%)
  between operations  14.2 us (14%)
  matrix products  11.7 us (12%)
  local copies, waits for them, and re-layouts  6.65 us (7%)
  other arithmetic  1.83 us (2%)
    reduce_scatter x1, waiting for transfers between devices, body(): lax.psum_scatter(value_grad.astype(jnp.bfloat16), 'frame', scatter_dimens...  38.6 us
    all_to_all x1, starting transfers between devices, body(): lax.all_to_all(inputs, 'frame', split_axis=1, concat_axis=0, tiled=True)  5.41 us
    unnamed x9, local copies, waits for them, and re-layouts  4.97 us
    ppermute x1, starting transfers between devices, shifted(): return lax.ppermute(shard, axis, pairs)  4.42 us
    ppermute x3, starting transfers between devices, body(): lax.ppermute(sent, 'frame', [(i_2, i_2 ^ step) for i_2 in range(size)])  3.61 us
    all_to_all x1, starting transfers between devices, body(): lax.all_to_all(upstream, 'frame', split_axis=1, concat_axis=0, tiled=True)  3.3 us
    ppermute x1, waiting for transfers between devices, shifted(): return lax.ppermute(shard, axis, pairs)  3.17 us
    all_to_all x1, waiting for transfers between devices, body(): lax.all_to_all(inputs, 'frame', split_axis=1, concat_axis=0, tiled=True)  3.11 us
  transfers between devices with their start and end apart: 8, of which 6 were waited for; matrix products, arithmetic and copies ran while one was open for 11% of the time, Pallas kernels for 0%

profile of v1, /device:TPU:1, one launch (start us, length us, event | category | flops | bytes accessed | tf_op | source)
XLA Modules:
  0.0 99.8 jit_solution(3172736112007728125)
XLA Ops:
  7.2 1.7 %copy.78 = bf16[1,1,8,4,1280]{4,2,3,1,0:T(8,128)(2,1)} copy(bf16[1,1,8,4,1280]{4,3,2,1,0:T(4,128)(2,1)} %param.6) | data formatting | bytes 163840 | tf_op args[0]
  8.9 5.4 %all-to-all-start.1 = ((bf16[8,4,1280]{2,0,1:T(8,128)(2,1)}), bf16[8,4,1280]{2,0,1:T(8,128)(2,1)S(1)}, u32[]{:S(2)}, u32[]{:S(2)}) async-start(bf16[8,4,1280]{2,0,1:T(8,128)(2,1)} %bitcast.100), calls=%async_computation.1 | async-start | bytes 163840 | tf_op jit(solution)/shard_map/all_to_all | solution.py:86
  14.3 1.5 %copy.79 = bf16[1,1,8,4,1280]{4,2,3,1,0:T(8,128)(2,1)} copy(bf16[1,1,8,4,1280]{4,3,2,1,0:T(4,128)(2,1)} %param.7) | data formatting | bytes 163840 | tf_op args[1]
  15.8 3.1 %all-to-all-done.1 = bf16[8,4,1280]{2,0,1:T(8,128)(2,1)S(1)} async-done(((bf16[8,4,1280]{2,0,1:T(8,128)(2,1)}), bf16[8,4,1280]{2,0,1:T(8,128)(2,1)S(1)}, u32[]{:S(2)}, u32[]{:S(2)}) %all-to-all-start.1) | async-done | bytes 81952 | tf_op jit(solution)/shard_map/all_to_all | solution.py:86
  18.9 3.3 %all-to-all-start = ((bf16[8,4,1280]{2,0,1:T(8,128)(2,1)}), bf16[8,4,1280]{2,0,1:T(8,128)(2,1)S(1)}, u32[]{:S(2)}, u32[]{:S(2)}) async-start(bf16[8,4,1280]{2,0,1:T(8,128)(2,1)} %bitcast.101), calls=%async_computation | async-start | bytes 163840 | tf_op jit(solution)/shard_map/all_to_all | solution.py:87
  22.3 0.5 fusion.29
  22.7 1.1 %copy-done.1 = bf16[1,1280,768]{2,1,0:T(8,128)(2,1)S(1)} copy-done((bf16[1,1280,768]{2,1,0:T(8,128)(2,1)S(1)}, bf16[1,1280,768]{2,1,0:T(8,128)(2,1)}, u32[]{:S(2)}) %copy-start.1) | copy-done | bytes 1966104
  23.8 0.5 fusion.26
  24.3 0.1 reshape.146
  24.6 2.2 %all-to-all-done = bf16[8,4,1280]{2,0,1:T(8,128)(2,1)S(1)} async-done(((bf16[8,4,1280]{2,0,1:T(8,128)(2,1)}), bf16[8,4,1280]{2,0,1:T(8,128)(2,1)S(1)}, u32[]{:S(2)}, u32[]{:S(2)}) %all-to-all-start) | async-done | bytes 81952 | tf_op jit(solution)/shard_map/all_to_all | solution.py:87
  26.8 2.0 %fusion.32 = bf16[32,768]{1,0:T(8,128)(2,1)S(1)} fusion(bf16[1,1280,768]{2,1,0:T(8,128)(2,1)} %param.11, bf16[8,4,1280]{2,0,1:T(8,128)(2,1)S(1)} %all-to-all-done), kind=kOutput, calls=%fused_computation.36 | convolution fusion | flops 62939136 | bytes 2097152 | tf_op jit(solution)/shard_map/dot_general | solution.py:89
  29.0 0.2 fusion.63
  29.2 0.2 fusion.23
  29.5 2.0 %fusion.1 = bf16[1280,768]{0,1:T(8,128)(2,1)} fusion(bf16[32,768]{1,0:T(8,128)(2,1)S(1)} %reshape.152, bf16[8,4,1280]{2,0,1:T(8,128)(2,1)S(1)} %all-to-all-done.1), kind=kOutput, calls=%fused_computation.3 | convolution fusion | flops 63897600 | bytes 2097152 | tf_op jit(solution)/shard_map/fpc,fpj->cj/dot_general | solution.py:74
  31.6 2.0 %fusion.35 = bf16[32,768]{1,0:T(8,128)(2,1)S(1)} fusion(bf16[1,1280,768]{2,1,0:T(8,128)(2,1)} %param.10, bf16[8,4,1280]{2,0,1:T(8,128)(2,1)S(1)} %all-to-all-done.1), kind=kOutput, calls=%fused_computation.37 | convolution fusion | flops 62939136 | bytes 2097152 | tf_op jit(solution)/shard_map/dot_general | solution.py:33
  33.8 0.2 multiply_reduce_fusion
  34.1 0.2 fusion.25
  34.5 0.2 fusion.24
  34.8 0.7 fusion.12
  35.5 38.6 %reduce-scatter.3.cloned.1.call-done = bf16[1280,192]{0,1:T(8,128)(2,1)} async-done(((bf16[1280,768]{0,1:T(8,128)(2,1)}), bf16[1280,192]{0,1:T(8,128)(2,1)}) %reduce-scatter.3.cloned.1.call-update) | async-done | bytes 491536 | tf_op jit(solution)/shard_map/reduce_scatter | solution.py:105
  74.2 2.4 %convolution_add_fusion.1 = f32[32,1280]{1,0:T(8,128)S(1)} fusion(f32[32,1280]{1,0:T(8,128)S(1)} %fusion.12, bf16[32,768]{1,0:T(8,128)(2,1)S(1)} %reshape.151, bf16[1,1280,768]{2,1,0:T(8,128)(2,1)} %param.9), kind=kOutput, calls=%fused_computation.5 | convolution fusion | flops 62955520 | bytes 2342912 | tf_op jit(solution)/shard_map/fpj,cj->fpc/dot_general | solution.py:69
  76.6 0.7 fusion.6
  77.3 1.5 %collective-permute-start.2 = (bf16[8,1,1280]{2,0,1:T(8,128)(2,1)S(1)}, bf16[8,1,1280]{2,0,1:T(8,128)(2,1)S(1)}, u32[]{:S(2)}, u32[]{:S(2)}) collective-permute-start(bf16[8,1,1280]{2,0,1:T(8,128)(2,1)S(1)} %get-tuple-element.7), channel_id=1, source_target_pairs={{0,24},{8,16},{16,8},{24,0},{1,25},{9,17},{17,9},{25,1},{2,26},{10... | collective-permute-start | bytes 61448 | tf_op jit(solution)/shard_map/ppermute | solution.py:101
  78.8 0.3 collective-permute-start.1
  79.1 1.9 %collective-permute-start = (bf16[8,1,1280]{2,0,1:T(8,128)(2,1)S(1)}, bf16[8,1,1280]{2,0,1:T(8,128)(2,1)S(1)}, u32[]{:S(2)}, u32[]{:S(2)}) collective-permute-start(bf16[8,1,1280]{2,0,1:T(8,128)(2,1)S(1)} %get-tuple-element.9), channel_id=1, source_target_pairs={{0,8},{8,0},{16,24},{24,16},{1,9},{9,1},{17,25},{25,17},{2,10},{10... | collective-permute-start | bytes 61448 | tf_op jit(solution)/shard_map/ppermute | solution.py:101
  81.0 0.9 collective-permute-done.2
  81.8 0.5 collective-permute-done.1
  82.4 0.6 gather_fusion
  82.9 4.4 %collective-permute-start.3 = (bf16[1,1,8,4,1280]{4,2,3,1,0:T(8,128)(2,1)S(1)}, bf16[1,1,8,4,1280]{4,2,3,1,0:T(8,128)(2,1)S(1)}, u32[]{:S(2)}, u32[]{:S(2)}) collective-permute-start(bf16[1,1,8,4,1280]{4,2,3,1,0:T(8,128)(2,1)S(1)} %bitcast.102), channel_id=1, source_target_pairs={{2,0},{4,2},{6,4},{3,1},{5,3},{7,5},{10,8},{12,10},{14,12},{11,9},... | collective-permute-start | bytes 245768 | tf_op jit(solution)/shard_map/ppermute | solution.py:25
  87.4 3.2 %collective-permute-done.3 = bf16[1,1,8,4,1280]{4,2,3,1,0:T(8,128)(2,1)S(1)} collective-permute-done((bf16[1,1,8,4,1280]{4,2,3,1,0:T(8,128)(2,1)S(1)}, bf16[1,1,8,4,1280]{4,2,3,1,0:T(8,128)(2,1)S(1)}, u32[]{:S(2)}, u32[]{:S(2)}) %collective-permute-start.3) | collective-permute-done | bytes 81952 | tf_op jit(solution)/shard_map/ppermute | solution.py:25
  90.5 0.7 copy.44
  91.2 1.8 %bitcast_convert_fusion = f32[1,1280,96]{1,2,0:T(8,128)} fusion(bf16[1280,96]{0,1:T(8,128)(2,1)} %reduce-scatter.5.cloned.1.call-done), kind=kLoop, calls=%fused_computation.38 | loop fusion | flops 122880 | bytes 737280 | tf_op jit(solution)/shard_map/broadcast_in_dim | solution.py:111
  (25 shorter events, 1.2 us)
Async XLA Ops:
  7.2 15.1 %copy-start = (bf16[1,1280,768]{2,1,0:T(8,128)(2,1)S(1)}, bf16[1,1280,768]{2,1,0:T(8,128)(2,1)}, u32[]{:S(2)}) copy-start(bf16[1,1280,768]{2,1,0:T(8,128)(2,1)} %param.8) | copy-start | bytes 5898244
  8.9 10.0 %all-to-all-start.1 = ((bf16[8,4,1280]{2,0,1:T(8,128)(2,1)}), bf16[8,4,1280]{2,0,1:T(8,128)(2,1)S(1)}, u32[]{:S(2)}, u32[]{:S(2)}) async-start(bf16[8,4,1280]{2,0,1:T(8,128)(2,1)} %bitcast.100), calls=%async_computation.1 | async-start | bytes 163840 | tf_op jit(solution)/shard_map/all_to_all | solution.py:86
  18.9 7.9 %all-to-all-start = ((bf16[8,4,1280]{2,0,1:T(8,128)(2,1)}), bf16[8,4,1280]{2,0,1:T(8,128)(2,1)S(1)}, u32[]{:S(2)}, u32[]{:S(2)}) async-start(bf16[8,4,1280]{2,0,1:T(8,128)(2,1)} %bitcast.101), calls=%async_computation | async-start | bytes 163840 | tf_op jit(solution)/shard_map/all_to_all | solution.py:87
  22.2 52.0 %reduce-scatter.3.cloned.1.call-start = ((), (), s32[]{:S(2)}) async-start(), calls=%async_computation.4 | async-start | bytes 2457600 | tf_op jit(solution)/shard_map/reduce_scatter | solution.py:105
  22.3 1.5 %copy-start.1 = (bf16[1,1280,768]{2,1,0:T(8,128)(2,1)S(1)}, bf16[1,1280,768]{2,1,0:T(8,128)(2,1)}, u32[]{:S(2)}) copy-start(bf16[1,1280,768]{2,1,0:T(8,128)(2,1)} %param.9) | copy-start | bytes 5898244
  31.6 59.6 %reduce-scatter.5.cloned.1.call-start = ((), (), s32[]{:S(2)}) async-start(), calls=%async_computation.5 | async-start | bytes 737280 | tf_op jit(solution)/shard_map/reduce_scatter | solution.py:108
  74.2 2.4 %copy-start.2 = (bf16[1,1280,768]{2,1,0:T(8,128)(2,1)S(1)}, bf16[1,1280,768]{2,1,0:T(8,128)(2,1)}, u32[]{:S(2)}) copy-start(bf16[1,1280,768]{2,1,0:T(8,128)(2,1)} %param.10) | copy-start | bytes 5898244
  77.3 4.5 %collective-permute-start.2 = (bf16[8,1,1280]{2,0,1:T(8,128)(2,1)S(1)}, bf16[8,1,1280]{2,0,1:T(8,128)(2,1)S(1)}, u32[]{:S(2)}, u32[]{:S(2)}) collective-permute-start(bf16[8,1,1280]{2,0,1:T(8,128)(2,1)S(1)} %get-tuple-element.7), channel_id=1, source_target_pairs={{0,24},{8,16},{16,8},{24,0},{1,25},{9,17},{17,9},{25,1},{2,26},{10... | collective-permute-start | bytes 61448 | tf_op jit(solution)/shard_map/ppermute | solution.py:101
  78.8 3.5 %collective-permute-start.1 = (bf16[8,1,1280]{2,0,1:T(8,128)(2,1)S(1)}, bf16[8,1,1280]{2,0,1:T(8,128)(2,1)S(1)}, u32[]{:S(2)}, u32[]{:S(2)}) collective-permute-start(bf16[8,1,1280]{2,0,1:T(8,128)(2,1)S(1)} %get-tuple-element.8), channel_id=1, source_target_pairs={{0,16},{8,24},{16,0},{24,8},{1,17},{9,25},{17,1},{25,9},{2,18},{10... | collective-permute-start | bytes 61448 | tf_op jit(solution)/shard_map/ppermute | solution.py:101
  79.1 3.3 %collective-permute-start = (bf16[8,1,1280]{2,0,1:T(8,128)(2,1)S(1)}, bf16[8,1,1280]{2,0,1:T(8,128)(2,1)S(1)}, u32[]{:S(2)}, u32[]{:S(2)}) collective-permute-start(bf16[8,1,1280]{2,0,1:T(8,128)(2,1)S(1)} %get-tuple-element.9), channel_id=1, source_target_pairs={{0,8},{8,0},{16,24},{24,16},{1,9},{9,1},{17,25},{25,17},{2,10},{10... | collective-permute-start | bytes 61448 | tf_op jit(solution)/shard_map/ppermute | solution.py:101
  82.9 7.6 %collective-permute-start.3 = (bf16[1,1,8,4,1280]{4,2,3,1,0:T(8,128)(2,1)S(1)}, bf16[1,1,8,4,1280]{4,2,3,1,0:T(8,128)(2,1)S(1)}, u32[]{:S(2)}, u32[]{:S(2)}) collective-permute-start(bf16[1,1,8,4,1280]{4,2,3,1,0:T(8,128)(2,1)S(1)} %bitcast.102), channel_id=1, source_target_pairs={{2,0},{4,2},{6,4},{3,1},{5,3},{7,5},{10,8},{12,10},{14,12},{11,9},... | collective-permute-start | bytes 245768 | tf_op jit(solution)/shard_map/ppermute | solution.py:25
Sparse Core Ops, SparseCore 0:
  31.7 42.4 reduce-scatter.2
  76.4 13.5 reduce-scatter.4
